TPU v7x, 32 devices: a whole 2x2x4 slice. The times are simulated.
32 devices in a mesh: pair: 16 (over z, y, x), rep: 2 (over core).
Axes of the slice: x: 2, y: 2, z: 4, core: 2. Of those that a mesh axis runs over, the one named last changes fastest.
Arguments:
- triplet_pairs: int32 [256, 3], P(('pair', 'rep')), may hold values from 0 to 1023, as said below
- tno_width: int32 [256], P(('pair', 'rep')), may hold values from 64 to 128
- pair_width: int32 [1024], P('pair'), may hold values from 32 to 64
- pair_coeff: bfloat16 [1024, 64, 1024], P('pair'), may hold values from -0.1875 to 0.1875
- pair_amps: bfloat16 [1024, 64, 64], P('pair'), may hold values from -0.03125 to 0.03125
- pair_exch: bfloat16 [1024, 64, 64], P('pair'), may hold values from -0.3125 to 0.3125
- tno_coeff: bfloat16 [256, 1024, 128], P(('pair', 'rep')), may hold values from -0.1875 to 0.1875
- int_left: bfloat16 [256, 3, 128, 128], P(('pair', 'rep')), may hold values from -6 to 6
- int_right: bfloat16 [256, 3, 128, 128], P(('pair', 'rep')), may hold values from -6 to 6
- singles: float32 [256, 3, 128], P(('pair', 'rep')), may hold values from -6 to 6
- tno_energy: float32 [256, 128], P(('pair', 'rep')), may hold values from 0.5 to 5
- gap: float32 [256], P(('pair', 'rep')), may hold values from 1 to 4
Outputs:
- triplet_energy: float32 [256], P(('pair', 'rep'))
- pair_energy: float32 [1024], P('pair')
Inputs may be any that keep to these rules, and one draw needn't show every extreme that they name: `triplet_pairs`: pair p is owned by index p // 64 of axis pair. The triplets of one chip are rows 2 * c * 8 to 2 * (c + 1) * 8 - 1; among their 48 pair ids at most 3 have one owner, and in every chip some owner has exactly 3 of them.
All inputs are finite; a program needn't handle non-finite values.
Results may differ from a plain program's by a relative error of at most 0.00044.
Values may be sent and summed in bfloat16 or wider, within the bound.
A program may use at most 128 MiB of HBM per device.

v0:
```python
import jax
import jax.numpy as jnp
from jax import lax
from jax.sharding import PartitionSpec as P


def projected_energy(
    pno_coeff, pno_blocks, tno_block, tno_count, left, right, single_amps, tno_levels, shift
):
    tno_size = tno_block.shape[1]
    pno_size = pno_coeff.shape[1]
    kept_cols = (jnp.arange(tno_size, dtype=jnp.int32) < tno_count).astype(jnp.float32)
    tno_kept = tno_block * kept_cols.astype(jnp.bfloat16)[None, :]
    intersection = jnp.einsum(
        "xad,db->xab", pno_coeff, tno_kept, preferred_element_type=jnp.float32
    ).astype(jnp.bfloat16)
    halfway = jnp.einsum(
        "xab,xac->xbc", intersection, pno_blocks, preferred_element_type=jnp.float32
    ).astype(jnp.bfloat16)
    halfway = halfway.reshape(3, tno_size, 2, pno_size)
    projected = jnp.einsum(
        "xbkc,xcd->xkbd", halfway, intersection, preferred_element_type=jnp.float32
    )
    amps_tno = projected[:, 0].astype(jnp.bfloat16)
    exch_tno = projected[:, 1]
    left_cols = jnp.transpose(left, (2, 0, 1)).reshape(tno_size, 3 * tno_size)
    right_cols = jnp.transpose(right, (2, 0, 1)).reshape(tno_size, 3 * tno_size)
    khatri = (left_cols[:, None, :] * right_cols[None, :, :]).reshape(
        tno_size * tno_size, 3 * tno_size
    )
    leading = jnp.transpose(amps_tno, (1, 0, 2)).reshape(tno_size, 3 * tno_size)
    connected = lax.dot_general(
        leading, khatri, (((1,), (1,)), ((), ())), preferred_element_type=jnp.float32
    )
    connected = connected.reshape(tno_size, tno_size, tno_size)
    complete = connected + single_amps[0][None, None, :] * exch_tno[0][:, :, None]
    complete = complete + single_amps[1][None, :, None] * exch_tno[1][:, None, :]
    complete = complete + single_amps[2][:, None, None] * exch_tno[2][None, :, :]
    denominator = (
        tno_levels[:, None, None] + tno_levels[None, :, None] + tno_levels[None, None, :] + shift
    )
    cube_mask = kept_cols[:, None, None] * kept_cols[None, :, None] * kept_cols[None, None, :]
    return jnp.sum(cube_mask * connected * complete / denominator)


def owner_ranks(owners):
    matching = owners[:, None] == owners[None, :]
    position = jnp.arange(owners.shape[0], dtype=jnp.int32)
    earlier = position[None, :] < position[:, None]
    return jnp.sum(jnp.logical_and(matching, earlier), axis=1)


def body(
    triplet_pairs,
    tno_width,
    pair_width,
    pair_coeff,
    pair_amps,
    pair_exch,
    tno_coeff,
    int_left,
    int_right,
    singles,
    tno_energy,
    gap,
):
    owner_count = lax.axis_size("pair")
    pair_dev = pair_coeff.shape[0]
    pno_size = pair_coeff.shape[1]
    domain = pair_coeff.shape[2]
    references = triplet_pairs.reshape(-1)
    ref_count = references.shape[0]
    capacity = (2 * ref_count + owner_count - 1) // owner_count
    kept_rows = (jnp.arange(pno_size, dtype=jnp.int32)[None, :] < pair_width[:, None]).astype(
        jnp.bfloat16
    )
    masked = pair_coeff * kept_rows[:, :, None]
    paired = jnp.concatenate([pair_amps, pair_exch], axis=2)
    chip_refs = lax.all_gather(references, "rep", axis=0, tiled=True)
    owners = chip_refs // pair_dev
    slot_rank = owner_ranks(owners)
    requests = (
        jnp.zeros((owner_count * capacity,), jnp.int32)
        .at[owners * capacity + slot_rank]
        .set(chip_refs % pair_dev)
    )
    requests = requests.reshape(owner_count, capacity)
    asked_rows = lax.all_to_all(requests, "pair", split_axis=0, concat_axis=0, tiled=True)
    replica = lax.axis_index("rep")
    coeff_part = lax.dynamic_slice_in_dim(masked, replica * (domain // 2), domain // 2, 2)
    paired_part = lax.dynamic_slice_in_dim(paired, replica * pno_size, pno_size, 2)
    got_coeff, got_paired = (
        lax.all_to_all(coeff_part[asked_rows], "pair", split_axis=0, concat_axis=0, tiled=True),
        lax.all_to_all(paired_part[asked_rows], "pair", split_axis=0, concat_axis=0, tiled=True),
    )
    got_coeff, got_paired = (
        lax.all_gather(got_coeff, "rep", axis=3, tiled=True),
        lax.all_gather(got_paired, "rep", axis=3, tiled=True),
    )
    positions = owners * capacity + slot_rank
    positions = lax.dynamic_slice_in_dim(positions, replica * ref_count, ref_count)
    flat_coeff = got_coeff.reshape(-1, pno_size, domain)
    flat_paired = got_paired.reshape(-1, pno_size, 2 * pno_size)
    trips = tno_coeff.shape[0]
    coeff_trip = flat_coeff[positions].reshape(trips, 3, pno_size, domain)
    paired_trip = flat_paired[positions].reshape(trips, 3, pno_size, 2 * pno_size)

    def single_triplet(items):
        return projected_energy(*items)

    energies = lax.map(
        single_triplet,
        (
            coeff_trip,
            paired_trip,
            tno_coeff,
            tno_width,
            int_left,
            int_right,
            singles,
            tno_energy,
            gap,
        ),
    )
    shares = jnp.repeat(energies / 3.0, 3)
    all_pairs = jnp.arange(owner_count * pair_dev, dtype=jnp.int32)
    dense = jnp.sum(
        jnp.where(references[:, None] == all_pairs[None, :], shares[:, None], 0.0), axis=0
    )
    owned = lax.psum_scatter(dense, "pair", scatter_dimension=0, tiled=True)
    pair_energy = lax.psum(owned, "rep")
    return (energies, pair_energy)


def solution(mesh):
    placed = (
        P(("pair", "rep"), None),
        P(("pair", "rep")),
        P("pair"),
        P("pair", None, None),
        P("pair", None, None),
        P("pair", None, None),
        P(("pair", "rep"), None, None),
        P(("pair", "rep"), None, None, None),
        P(("pair", "rep"), None, None, None),
        P(("pair", "rep"), None, None),
        P(("pair", "rep"), None),
        P(("pair", "rep")),
    )
    return jax.shard_map(
        body, mesh=mesh, in_specs=placed, out_specs=(P(("pair", "rep")), P("pair")), check_vma=False
    )
```

profile of v0, /device:TPU:0, one launch (start us, length us, event | category | flops | bytes accessed | tf_op | source)
XLA Modules:
  0.0 362.0 jit_solution(6125471141535542919)
XLA Ops:
  8.0 1.2 dynamic-slice
  10.2 2.0 all-reduce
  13.7 8.2 %all-to-all-start = ((s32[16,1,3]{2,1,0:T(1,128)}), s32[16,1,3]{2,1,0:T(1,128)S(1)}, u32[]{:S(2)}, u32[]{:S(2)}) async-start(s32[16,1,3]{2,1,0:T(1,128)} %bitcast.29), calls=%async_computation | async-start | bytes 16384 | tf_op jit(solution)/shard_map/all_to_all | solution.py:88
  22.7 4.0 %dynamic-slice_multiply_fusion = bf16[64,64,512]{2,1,0:T(8,128)(2,1)} fusion(bf16[64,64,1024]{2,1,0:T(8,128)(2,1)} %param.17, s32[]{:T(128)S(6)} %select_n.43, bf16[64,64]{1,0:T(8,128)(2,1)S(1)} %fusion.23), kind=kLoop, calls=%fused_computation.43 | loop fusion | flops 8388608 | bytes 8396804 | tf_op jit(solution)/shard_map/mul | solution.py:77
  26.7 2.5 all-to-all-done
  29.5 2.9 gather_fusion
  32.5 75.4 %all_to_all.22 = bf16[16,3,64,512]{3,2,1,0:T(8,128)(2,1)} all-to-all(bf16[16,3,64,512]{3,2,1,0:T(8,128)(2,1)S(1)} %bitcast.110), channel_id=1, replica_groups=mesh['pair'=16,'rep'=2] {'pair'}, dimensions={0} | all-to-all | bytes 6291456 | tf_op jit(solution)/shard_map/all_to_all | solution.py:93
  107.9 2.6 dynamic-slice_maximum_fusion
  111.2 1.3 reshape.272
  112.5 3.9 %all-to-all-start.2 = ((bf16[16,2,6144]{2,1,0:T(2,128)(2,1)}), bf16[16,2,6144]{2,1,0:T(2,128)(2,1)S(1)}, u32[]{:S(2)}, u32[]{:S(2)}) async-start(bf16[16,2,6144]{2,1,0:T(2,128)(2,1)} %reshape.272), calls=%async_computation.2 | async-start | bytes 786432 | tf_op jit(solution)/shard_map/all_to_all | solution.py:94
  117.8 10.5 %all-to-all-done.2 = bf16[16,2,6144]{2,1,0:T(2,128)(2,1)S(1)} async-done(((bf16[16,2,6144]{2,1,0:T(2,128)(2,1)}), bf16[16,2,6144]{2,1,0:T(2,128)(2,1)S(1)}, u32[]{:S(2)}, u32[]{:S(2)}) %all-to-all-start.2) | async-done | bytes 393248 | tf_op jit(solution)/shard_map/all_to_all | solution.py:94
  129.5 2.9 all_gather.11
  132.4 1.2 copy.64
  133.6 1.4 gather_fusion.3
  134.9 3.5 gather_fusion.1
  138.5 174.5 %while.10 = (s32[]{:T(128)}, f32[8]{0:T(128)S(1)}, s32[8]{0:T(128)S(1)}, bf16[8,3,64,1024]{3,2,1,0:T(8,128)(2,1)S(1)}, bf16[8,1024,128]{2,1,0:T(8,128)(2,1)}, /*...) while((s32[]{:T(128)}, f32[8]{0:T(128)S(1)}, ...), condition=%wide.region_4.5_spmd, body=%wide.region_2.4_spmd.sunk | while | flops 1732485504 | bytes 29010464 | solution.py:111
  139.9 1.2 convolution_convert_fusion.4
  141.1 1.0 convolution_convert_fusion.5
  143.9 1.0 constant_dynamic-slice_fusion.7
  147.9 11.6 %fusion.51 = f32[]{:T(128)} fusion(f32[]{:T(128)} %bitcast.103, f32[128]{0:T(128)S(1)} %fusion.49, f32[128,128]{0,1:T(8,128)S(1)} %broadcast_add_fusion.2, f32[128,128]{1,0:T(8,128)S(1)} %copy.77, f32[128]{0:T(128)S(1)} %get-tuple-element.230, f32[128,128]{1,0:T(8,128)} %copy.78, f32[128]{0:T(128)S(1)} %get-tuple-element.232, ...), kind=kOutput, calls=%fused_computation.8.clone.1 | convolution fusion | flops 1663041536 | bytes 625160 | tf_op jit(solution)/shard_map/while/body/eval_jaxpr/dot_general | solution.py:32
  161.7 1.2 convolution_convert_fusion.4
  162.9 1.0 convolution_convert_fusion.5
  165.7 1.0 constant_dynamic-slice_fusion.7
  169.8 11.6 %fusion.51 = f32[]{:T(128)} fusion(f32[]{:T(128)} %bitcast.103, f32[128]{0:T(128)S(1)} %fusion.49, f32[128,128]{0,1:T(8,128)S(1)} %broadcast_add_fusion.2, f32[128,128]{1,0:T(8,128)S(1)} %copy.77, f32[128]{0:T(128)S(1)} %get-tuple-element.230, f32[128,128]{1,0:T(8,128)} %copy.78, f32[128]{0:T(128)S(1)} %get-tuple-element.232, ...), kind=kOutput, calls=%fused_computation.8.clone.1 | convolution fusion | flops 1663041536 | bytes 625160 | tf_op jit(solution)/shard_map/while/body/eval_jaxpr/dot_general | solution.py:32
  183.5 1.2 convolution_convert_fusion.4
  184.7 1.0 convolution_convert_fusion.5
  187.5 1.0 constant_dynamic-slice_fusion.7
  191.6 11.6 %fusion.51 = f32[]{:T(128)} fusion(f32[]{:T(128)} %bitcast.103, f32[128]{0:T(128)S(1)} %fusion.49, f32[128,128]{0,1:T(8,128)S(1)} %broadcast_add_fusion.2, f32[128,128]{1,0:T(8,128)S(1)} %copy.77, f32[128]{0:T(128)S(1)} %get-tuple-element.230, f32[128,128]{1,0:T(8,128)} %copy.78, f32[128]{0:T(128)S(1)} %get-tuple-element.232, ...), kind=kOutput, calls=%fused_computation.8.clone.1 | convolution fusion | flops 1663041536 | bytes 625160 | tf_op jit(solution)/shard_map/while/body/eval_jaxpr/dot_general | solution.py:32
  205.3 1.2 convolution_convert_fusion.4
  206.5 1.0 convolution_convert_fusion.5
  209.3 1.0 constant_dynamic-slice_fusion.7
  213.4 11.6 %fusion.51 = f32[]{:T(128)} fusion(f32[]{:T(128)} %bitcast.103, f32[128]{0:T(128)S(1)} %fusion.49, f32[128,128]{0,1:T(8,128)S(1)} %broadcast_add_fusion.2, f32[128,128]{1,0:T(8,128)S(1)} %copy.77, f32[128]{0:T(128)S(1)} %get-tuple-element.230, f32[128,128]{1,0:T(8,128)} %copy.78, f32[128]{0:T(128)S(1)} %get-tuple-element.232, ...), kind=kOutput, calls=%fused_computation.8.clone.1 | convolution fusion | flops 1663041536 | bytes 625160 | tf_op jit(solution)/shard_map/while/body/eval_jaxpr/dot_general | solution.py:32
  227.1 1.2 convolution_convert_fusion.4
  228.3 1.0 convolution_convert_fusion.5
  235.2 11.6 %fusion.51 = f32[]{:T(128)} fusion(f32[]{:T(128)} %bitcast.103, f32[128]{0:T(128)S(1)} %fusion.49, f32[128,128]{0,1:T(8,128)S(1)} %broadcast_add_fusion.2, f32[128,128]{1,0:T(8,128)S(1)} %copy.77, f32[128]{0:T(128)S(1)} %get-tuple-element.230, f32[128,128]{1,0:T(8,128)} %copy.78, f32[128]{0:T(128)S(1)} %get-tuple-element.232, ...), kind=kOutput, calls=%fused_computation.8.clone.1 | convolution fusion | flops 1663041536 | bytes 625160 | tf_op jit(solution)/shard_map/while/body/eval_jaxpr/dot_general | solution.py:32
  248.9 1.2 convolution_convert_fusion.4
  250.2 1.0 convolution_convert_fusion.5
  253.0 1.0 constant_dynamic-slice_fusion.7
  257.0 11.6 %fusion.51 = f32[]{:T(128)} fusion(f32[]{:T(128)} %bitcast.103, f32[128]{0:T(128)S(1)} %fusion.49, f32[128,128]{0,1:T(8,128)S(1)} %broadcast_add_fusion.2, f32[128,128]{1,0:T(8,128)S(1)} %copy.77, f32[128]{0:T(128)S(1)} %get-tuple-element.230, f32[128,128]{1,0:T(8,128)} %copy.78, f32[128]{0:T(128)S(1)} %get-tuple-element.232, ...), kind=kOutput, calls=%fused_computation.8.clone.1 | convolution fusion | flops 1663041536 | bytes 625160 | tf_op jit(solution)/shard_map/while/body/eval_jaxpr/dot_general | solution.py:32
  270.7 1.2 convolution_convert_fusion.4
  272.0 1.0 convolution_convert_fusion.5
  274.8 1.0 constant_dynamic-slice_fusion.7
  278.8 11.6 %fusion.51 = f32[]{:T(128)} fusion(f32[]{:T(128)} %bitcast.103, f32[128]{0:T(128)S(1)} %fusion.49, f32[128,128]{0,1:T(8,128)S(1)} %broadcast_add_fusion.2, f32[128,128]{1,0:T(8,128)S(1)} %copy.77, f32[128]{0:T(128)S(1)} %get-tuple-element.230, f32[128,128]{1,0:T(8,128)} %copy.78, f32[128]{0:T(128)S(1)} %get-tuple-element.232, ...), kind=kOutput, calls=%fused_computation.8.clone.1 | convolution fusion | flops 1663041536 | bytes 625160 | tf_op jit(solution)/shard_map/while/body/eval_jaxpr/dot_general | solution.py:32
  292.6 1.2 convolution_convert_fusion.4
  293.8 1.0 convolution_convert_fusion.5
  300.6 11.6 %fusion.51 = f32[]{:T(128)} fusion(f32[]{:T(128)} %bitcast.103, f32[128]{0:T(128)S(1)} %fusion.49, f32[128,128]{0,1:T(8,128)S(1)} %broadcast_add_fusion.2, f32[128,128]{1,0:T(8,128)S(1)} %copy.77, f32[128]{0:T(128)S(1)} %get-tuple-element.230, f32[128,128]{1,0:T(8,128)} %copy.78, f32[128]{0:T(128)S(1)} %get-tuple-element.232, ...), kind=kOutput, calls=%fused_computation.8.clone.1 | convolution fusion | flops 1663041536 | bytes 625160 | tf_op jit(solution)/shard_map/while/body/eval_jaxpr/dot_general | solution.py:32
  313.3 38.8 %all-reduce.1 = f32[1024]{0:T(1024)S(1)} all-reduce(f32[1024]{0:T(1024)S(1)} %select_reduce_fusion), channel_id=2, replica_groups=mesh['pair'=16,'rep'=2] {'pair'}, use_global_device_ids=true, to_apply=%region_6.7.clone | all-reduce | flops 1024 | bytes 8192
  352.2 2.9 psum.7
  (192 shorter events, 63.6 us)
Async XLA Ops:
  13.7 15.5 %all-to-all-start = ((s32[16,1,3]{2,1,0:T(1,128)}), s32[16,1,3]{2,1,0:T(1,128)S(1)}, u32[]{:S(2)}, u32[]{:S(2)}) async-start(s32[16,1,3]{2,1,0:T(1,128)} %bitcast.29), calls=%async_computation | async-start | bytes 16384 | tf_op jit(solution)/shard_map/all_to_all | solution.py:88
  21.9 113.0 %all-gather.2.cloned.1.call-start = ((), (), s32[]{:S(2)}) async-start(), calls=%async_computation.3 | async-start | bytes 9437184 | tf_op jit(solution)/shard_map/all_gather | solution.py:97
  32.5 84.0 %copy-start.4 = (u32[32]{0:T(128)S(1)}, u32[32]{0:T(128)}, u32[]{:S(2)}) copy-start(u32[32]{0:T(128)} %constant.93) | copy-start | bytes 388
  111.2 27.3 %copy-start.2 = (s32[8]{0:T(128)S(1)}, s32[8]{0:T(128)}, u32[]{:S(2)}) copy-start(s32[8]{0:T(128)} %param.15) | copy-start | bytes 100
  111.2 27.3 %copy-start.3 = (f32[8]{0:T(128)S(1)}, f32[8]{0:T(128)}, u32[]{:S(2)}) copy-start(f32[8]{0:T(128)} %param.25) | copy-start | bytes 100
  112.5 15.8 %all-to-all-start.2 = ((bf16[16,2,6144]{2,1,0:T(2,128)(2,1)}), bf16[16,2,6144]{2,1,0:T(2,128)(2,1)S(1)}, u32[]{:S(2)}, u32[]{:S(2)}) async-start(bf16[16,2,6144]{2,1,0:T(2,128)(2,1)} %reshape.272), calls=%async_computation.2 | async-start | bytes 786432 | tf_op jit(solution)/shard_map/all_to_all | solution.py:94
  138.5 3.6 %copy-start = (bf16[8,3,64,1024]{3,2,1,0:T(8,128)(2,1)}, bf16[8,3,64,1024]{3,2,1,0:T(8,128)(2,1)S(1)}, u32[]{:S(2)}) copy-start(bf16[8,3,64,1024]{3,2,1,0:T(8,128)(2,1)S(1)} %get-tuple-element.271) | copy-start | bytes 9437188 | tf_op jit(solution)/shard_map/while
  147.9 12.4 %copy-start.1 = (bf16[8,3,64,1024]{3,2,1,0:T(8,128)(2,1)S(1)}, bf16[8,3,64,1024]{3,2,1,0:T(8,128)(2,1)}, u32[]{:S(2)}) copy-start(bf16[8,3,64,1024]{3,2,1,0:T(8,128)(2,1)} %copy-done) | copy-start | bytes 9437188 | tf_op jit(solution)/shard_map/while
  160.3 3.6 copy-start
  169.8 12.4 %copy-start.1 = (bf16[8,3,64,1024]{3,2,1,0:T(8,128)(2,1)S(1)}, bf16[8,3,64,1024]{3,2,1,0:T(8,128)(2,1)}, u32[]{:S(2)}) copy-start(bf16[8,3,64,1024]{3,2,1,0:T(8,128)(2,1)} %copy-done) | copy-start | bytes 9437188 | tf_op jit(solution)/shard_map/while
  182.2 3.6 copy-start
  191.6 12.4 %copy-start.1 = (bf16[8,3,64,1024]{3,2,1,0:T(8,128)(2,1)S(1)}, bf16[8,3,64,1024]{3,2,1,0:T(8,128)(2,1)}, u32[]{:S(2)}) copy-start(bf16[8,3,64,1024]{3,2,1,0:T(8,128)(2,1)} %copy-done) | copy-start | bytes 9437188 | tf_op jit(solution)/shard_map/while
  204.0 3.6 copy-start
  213.4 12.4 %copy-start.1 = (bf16[8,3,64,1024]{3,2,1,0:T(8,128)(2,1)S(1)}, bf16[8,3,64,1024]{3,2,1,0:T(8,128)(2,1)}, u32[]{:S(2)}) copy-start(bf16[8,3,64,1024]{3,2,1,0:T(8,128)(2,1)} %copy-done) | copy-start | bytes 9437188 | tf_op jit(solution)/shard_map/while
  225.8 3.6 copy-start
  235.2 12.4 %copy-start.1 = (bf16[8,3,64,1024]{3,2,1,0:T(8,128)(2,1)S(1)}, bf16[8,3,64,1024]{3,2,1,0:T(8,128)(2,1)}, u32[]{:S(2)}) copy-start(bf16[8,3,64,1024]{3,2,1,0:T(8,128)(2,1)} %copy-done) | copy-start | bytes 9437188 | tf_op jit(solution)/shard_map/while
  247.6 3.6 copy-start
  257.0 12.4 %copy-start.1 = (bf16[8,3,64,1024]{3,2,1,0:T(8,128)(2,1)S(1)}, bf16[8,3,64,1024]{3,2,1,0:T(8,128)(2,1)}, u32[]{:S(2)}) copy-start(bf16[8,3,64,1024]{3,2,1,0:T(8,128)(2,1)} %copy-done) | copy-start | bytes 9437188 | tf_op jit(solution)/shard_map/while
  269.4 3.6 copy-start
  278.8 12.4 %copy-start.1 = (bf16[8,3,64,1024]{3,2,1,0:T(8,128)(2,1)S(1)}, bf16[8,3,64,1024]{3,2,1,0:T(8,128)(2,1)}, u32[]{:S(2)}) copy-start(bf16[8,3,64,1024]{3,2,1,0:T(8,128)(2,1)} %copy-done) | copy-start | bytes 9437188 | tf_op jit(solution)/shard_map/while
  291.2 3.6 copy-start
  300.6 12.4 %copy-start.1 = (bf16[8,3,64,1024]{3,2,1,0:T(8,128)(2,1)S(1)}, bf16[8,3,64,1024]{3,2,1,0:T(8,128)(2,1)}, u32[]{:S(2)}) copy-start(bf16[8,3,64,1024]{3,2,1,0:T(8,128)(2,1)} %copy-done) | copy-start | bytes 9437188 | tf_op jit(solution)/shard_map/while
  313.0 42.1 %copy-start.5 = (f32[8]{0:T(128)}, f32[8]{0:T(128)S(1)}, u32[]{:S(2)}) copy-start(f32[8]{0:T(128)S(1)} %get-tuple-element.57) | copy-start | bytes 100
Sparse Core Ops, SparseCore 0:
  108.0 15.0 all-gather.1
where the time goes:
time: 364 us; the launch traced here: 362 us
  blocking collectives  122 us (34%)
  matrix products  113 us (31%)
  local copies, waits for them, and re-layouts  65.8 us (18%)
  other arithmetic  19.6 us (5%)
  between operations  15.5 us (4%)
  waiting for transfers between devices  13 us (4%)
  starting transfers between devices  12.2 us (3%)
    dot_general x8, matrix products, projected_energy(): lax.dot_general(leading, khatri, (((1,), (1,)), ((), ())), preferred_elem...  93.2 us
    all_to_all x1, blocking collectives, body(): lax.all_to_all(coeff_part[asked_rows], 'pair', split_axis=0, concat_axis=...  75.4 us
    unnamed x2, blocking collectives  40.8 us
    dynamic_slice x24, local copies, waits for them, and re-layouts, body(): lax.map(single_triplet, (coeff_trip, paired_trip, tno_coeff, tno_width, i...  17.7 us
    mul x16, local copies, waits for them, and re-layouts, projected_energy(): single_amps[0][None, None, :] * exch_tno[0][:, :, None]  10.9 us
    all_to_all x1, waiting for transfers between devices, body(): lax.all_to_all(paired_part[asked_rows], 'pair', split_axis=0, concat_axis...  10.5 us
    dot_general x8, matrix products, projected_energy(): jnp.einsum('xad,db->xab', pno_coeff, tno_kept, preferred_element_type=jnp...  9.65 us
    dot_general x8, matrix products, projected_energy(): jnp.einsum('xab,xac->xbc', intersection, pno_blocks, preferred_element_ty...  8.29 us
  transfers between devices with their start and end apart: 3, of which 2 were waited for; matrix products, arithmetic and copies ran while one was open for 4% of the time, Pallas kernels for 0%

commit v1 on v0

--- a/solution.py
+++ b/solution.py
@@ -2,6 +2,29 @@
 import jax.numpy as jnp
 from jax import lax
 from jax.sharding import PartitionSpec as P
+
+
+def cut_along(x, dim, size):
+    shape = x.shape
+    pieces = x.reshape(*shape[:dim], size, shape[dim] // size, *shape[dim + 1 :])
+    return jnp.moveaxis(pieces, dim, 0)
+
+
+def laid_out(blocks, dim):
+    blocks = jnp.moveaxis(blocks, 0, dim)
+    lengths = blocks.shape
+    return blocks.reshape(*lengths[:dim], lengths[dim] * lengths[dim + 1], *lengths[dim + 2 :])
+
+
+def exchange_in_pairs(shard, axis, split_dim, concat_dim):
+    size, index = (lax.axis_size(axis), lax.axis_index(axis))
+    tiles = cut_along(shard, split_dim, size)
+    done = [tiles[index]]
+    for step in range(1, size):
+        sent = tiles[index ^ step]
+        done.append(lax.ppermute(sent, axis, [(i, i ^ step) for i in range(size)]))
+    tiles = jnp.stack(done)[index ^ jnp.arange(size)]
+    return laid_out(tiles, concat_dim)
 
 
 def projected_energy(
@@ -90,7 +113,7 @@
     coeff_part = lax.dynamic_slice_in_dim(masked, replica * (domain // 2), domain // 2, 2)
     paired_part = lax.dynamic_slice_in_dim(paired, replica * pno_size, pno_size, 2)
     got_coeff, got_paired = (
-        lax.all_to_all(coeff_part[asked_rows], "pair", split_axis=0, concat_axis=0, tiled=True),
+        exchange_in_pairs(coeff_part[asked_rows], "pair", 0, 0),
         lax.all_to_all(paired_part[asked_rows], "pair", split_axis=0, concat_axis=0, tiled=True),
     )
     got_coeff, got_paired = (

time: 364 us -> 376 us (1.033)
  blocking collectives: 122 us -> 46.9 us
  starting transfers between devices: 12.2 us -> 48.5 us
  waiting for transfers between devices: 13 us -> 48.2 us
  local copies, waits for them, and re-layouts: 65.8 us -> 82.3 us
    all_to_all x1 -> x0, blocking collectives: 75.4 us -> none  [body(): lax.all_to_all(coeff_part[asked_rows], 'pair', split_axis=0, concat_axis=...]
    ppermute x0 -> x15, waiting for transfers between devices: none -> 37.3 us  [exchange_in_pairs(): done.append(lax.ppermute(sent, axis, [(i, i ^ step) for i in range(size)]))]
    ppermute x0 -> x15, starting transfers between devices: none -> 25.3 us  [exchange_in_pairs(): done.append(lax.ppermute(sent, axis, [(i, i ^ step) for i in range(size)]))]
    unnamed x15 -> x32, local copies, waits for them, and re-layouts: 4.71 us -> 16.3 us
    all_to_all x1, starting transfers between devices: 3.95 us -> 15 us  [body(): lax.all_to_all(paired_part[asked_rows], 'pair', split_axis=0, concat_axis...]
    gather x0 -> x1, local copies, waits for them, and re-layouts: none -> 4.34 us  [exchange_in_pairs(): tiles = jnp.stack(done)[index ^ jnp.arange(size)]]
  transfers between devices with their start and end apart: 3 -> 18, of which waited for: 2 -> 10; matrix products, arithmetic and copies ran while one was open for 4% -> 6% of each run, Pallas kernels for 0% -> 0%
where the time goes in v1:
time: 376 us; the launch traced here: 374 us
  matrix products  113 us (30%)
  local copies, waits for them, and re-layouts  82.3 us (22%)
  starting transfers between devices  48.5 us (13%)
  waiting for transfers between devices  48.2 us (13%)
  blocking collectives  46.9 us (12%)
  other arithmetic  19.2 us (5%)
  between operations  15.6 us (4%)
    dot_general x8, matrix products, projected_energy(): lax.dot_general(leading, khatri, (((1,), (1,)), ((), ())), preferred_elem...  93 us
    unnamed x2, blocking collectives  41 us
    ppermute x15, waiting for transfers between devices, exchange_in_pairs(): done.append(lax.ppermute(sent, axis, [(i, i ^ step) for i in range(size)]))  37.3 us
    ppermute x15, starting transfers between devices, exchange_in_pairs(): done.append(lax.ppermute(sent, axis, [(i, i ^ step) for i in range(size)]))  25.3 us
    dynamic_slice x24, local copies, waits for them, and re-layouts, body(): lax.map(single_triplet, (coeff_trip, paired_trip, tno_coeff, tno_width, i...  17.8 us
    unnamed x32, local copies, waits for them, and re-layouts  16.3 us
    all_to_all x1, starting transfers between devices, body(): lax.all_to_all(paired_part[asked_rows], 'pair', split_axis=0, concat_axis...  15 us
    mul x16, local copies, waits for them, and re-layouts, projected_energy(): single_amps[0][None, None, :] * exch_tno[0][:, :, None]  10.9 us
  transfers between devices with their start and end apart: 18, of which 10 were waited for; matrix products, arithmetic and copies ran while one was open for 6% of the time, Pallas kernels for 0%

profile of v1, /device:TPU:0, one launch (start us, length us, event | category | flops | bytes accessed | tf_op | source)
XLA Modules:
  0.0 374.3 jit_solution(1430905789480775947)
XLA Ops:
  8.0 1.2 dynamic-slice.19
  10.2 2.0 all-reduce
  13.7 8.2 %all-to-all-start = ((s32[16,1,3]{2,1,0:T(1,128)}), s32[16,1,3]{2,1,0:T(1,128)S(1)}, u32[]{:S(2)}, u32[]{:S(2)}) async-start(s32[16,1,3]{2,1,0:T(1,128)} %bitcast.29), calls=%async_computation | async-start | bytes 16384 | tf_op jit(solution)/shard_map/all_to_all | solution.py:111
  22.8 4.0 %dynamic-slice_multiply_fusion = bf16[64,64,512]{2,1,0:T(8,128)(2,1)} fusion(bf16[64,64,1024]{2,1,0:T(8,128)(2,1)} %param.17, s32[]{:T(128)S(6)} %select_n.101, bf16[64,64]{1,0:T(8,128)(2,1)S(1)} %fusion.23), kind=kLoop, calls=%fused_computation.44 | loop fusion | flops 8388608 | bytes 8396804 | tf_op jit(solution)/shard_map/mul | solution.py:100
  26.9 2.4 all-to-all-done
  29.5 2.9 gather_fusion
  34.0 2.3 collective-permute-start.2
  37.0 1.5 collective-permute-start.4
  39.1 3.5 collective-permute-done
  43.4 2.5 collective-permute-start.6
  48.3 3.1 collective-permute-start.8
  52.2 2.3 collective-permute-done.4
  55.1 3.8 %collective-permute-done.5 = bf16[1,3,64,512]{3,2,1,0:T(8,128)(2,1)S(1)} collective-permute-done((bf16[1,3,64,512]{3,2,1,0:T(8,128)(2,1)S(1)}, bf16[1,3,64,512]{3,2,1,0:T(8,128)(2,1)S(1)}, u32[]{:S(2)}, u32[]{:S(2)}) %collective-permute-start.5) | collective-permute-done | bytes 196640 | tf_op jit(solution)/shard_map/ppermute | solution.py:25
  58.9 1.5 collective-permute-start.10
  61.1 2.2 collective-permute-done.6
  65.2 15.3 %collective-permute-done.7 = bf16[1,3,64,512]{3,2,1,0:T(8,128)(2,1)S(1)} collective-permute-done((bf16[1,3,64,512]{3,2,1,0:T(8,128)(2,1)S(1)}, bf16[1,3,64,512]{3,2,1,0:T(8,128)(2,1)S(1)}, u32[]{:S(2)}, u32[]{:S(2)}) %collective-permute-start.7) | collective-permute-done | bytes 196640 | tf_op jit(solution)/shard_map/ppermute | solution.py:25
  80.5 3.7 collective-permute-start.12
  86.0 2.5 collective-permute-start.13
  89.2 7.2 %collective-permute-done.9 = bf16[1,3,64,512]{3,2,1,0:T(8,128)(2,1)S(1)} collective-permute-done((bf16[1,3,64,512]{3,2,1,0:T(8,128)(2,1)S(1)}, bf16[1,3,64,512]{3,2,1,0:T(8,128)(2,1)S(1)}, u32[]{:S(2)}, u32[]{:S(2)}) %collective-permute-start.9) | collective-permute-done | bytes 196640 | tf_op jit(solution)/shard_map/ppermute | solution.py:25
  96.4 4.1 %collective-permute-start.14 = (bf16[1,3,64,512]{3,2,1,0:T(8,128)(2,1)S(1)}, bf16[1,3,64,512]{3,2,1,0:T(8,128)(2,1)S(1)}, u32[]{:S(2)}, u32[]{:S(2)}) collective-permute-start(bf16[1,3,64,512]{3,2,1,0:T(8,128)(2,1)S(1)} %get-tuple-element.149), channel_id=1, source_target_pairs={{0,30},{2,28},{4,26},{6,24},{8,22},{10,20},{12,18},{14,16},{16,14}... | collective-permute-start | bytes 589832 | tf_op jit(solution)/shard_map/ppermute | solution.py:25
  104.0 1.8 collective-permute-done.14
  106.5 4.3 %gather_fusion.1 = bf16[16,3,64,512]{3,2,1,0:T(8,128)(2,1)} fusion(bf16[16,3,64,512]{3,2,1,0:T(8,128)(2,1)} %bitcast.48, s32[1024]{0:T(1024)S(1)} %pad_clamp_fusion.1), kind=kCustom, calls=%fused_computation.1 | custom fusion | bytes 6291520 | tf_op jit(solution)/shard_map/gather | solution.py:26
  112.1 2.3 dynamic-slice_maximum_fusion
  115.1 1.3 reshape.335
  116.4 15.0 %all-to-all-start.1 = ((bf16[16,2,6144]{2,1,0:T(2,128)(2,1)}), bf16[16,2,6144]{2,1,0:T(2,128)(2,1)S(1)}, u32[]{:S(2)}, u32[]{:S(2)}) async-start(bf16[16,2,6144]{2,1,0:T(2,128)(2,1)} %reshape.335), calls=%async_computation.1 | async-start | bytes 786432 | tf_op jit(solution)/shard_map/all_to_all | solution.py:117
  132.8 8.5 %all-to-all-done.1 = bf16[16,2,6144]{2,1,0:T(2,128)(2,1)S(1)} async-done(((bf16[16,2,6144]{2,1,0:T(2,128)(2,1)}), bf16[16,2,6144]{2,1,0:T(2,128)(2,1)S(1)}, u32[]{:S(2)}, u32[]{:S(2)}) %all-to-all-start.1) | async-done | bytes 393248 | tf_op jit(solution)/shard_map/all_to_all | solution.py:117
  142.4 2.9 all_gather.11
  146.5 1.4 gather_fusion.4
  147.9 3.6 gather_fusion.2
  151.5 173.6 %while.10 = (s32[]{:T(128)}, f32[8]{0:T(128)S(1)}, s32[8]{0:T(128)S(1)}, bf16[8,3,64,1024]{3,2,1,0:T(8,128)(2,1)S(1)}, bf16[8,1024,128]{2,1,0:T(8,128)(2,1)}, /*...) while((s32[]{:T(128)}, f32[8]{0:T(128)S(1)}, ...), condition=%wide.region_4.5_spmd, body=%wide.region_2.4_spmd.sunk | while | flops 1732485504 | bytes 29010464 | solution.py:134
  152.9 1.2 convolution_convert_fusion.4
  160.9 11.6 %fusion.52 = f32[]{:T(128)} fusion(f32[]{:T(128)} %bitcast.138, f32[128]{0:T(128)S(1)} %fusion.50, f32[128,128]{0,1:T(8,128)S(1)} %broadcast_add_fusion.2, f32[128,128]{1,0:T(8,128)S(1)} %copy.77, f32[128]{0:T(128)S(1)} %get-tuple-element.245, f32[128,128]{1,0:T(8,128)} %copy.78, f32[128]{0:T(128)S(1)} %get-tuple-element.247, ...), kind=kOutput, calls=%fused_computation.9.clone.1 | convolution fusion | flops 1663041536 | bytes 625160 | tf_op jit(solution)/shard_map/while/body/eval_jaxpr/dot_general | solution.py:55
  174.6 1.2 convolution_convert_fusion.4
  182.6 11.6 %fusion.52 = f32[]{:T(128)} fusion(f32[]{:T(128)} %bitcast.138, f32[128]{0:T(128)S(1)} %fusion.50, f32[128,128]{0,1:T(8,128)S(1)} %broadcast_add_fusion.2, f32[128,128]{1,0:T(8,128)S(1)} %copy.77, f32[128]{0:T(128)S(1)} %get-tuple-element.245, f32[128,128]{1,0:T(8,128)} %copy.78, f32[128]{0:T(128)S(1)} %get-tuple-element.247, ...), kind=kOutput, calls=%fused_computation.9.clone.1 | convolution fusion | flops 1663041536 | bytes 625160 | tf_op jit(solution)/shard_map/while/body/eval_jaxpr/dot_general | solution.py:55
  196.3 1.2 convolution_convert_fusion.4
  204.3 11.6 %fusion.52 = f32[]{:T(128)} fusion(f32[]{:T(128)} %bitcast.138, f32[128]{0:T(128)S(1)} %fusion.50, f32[128,128]{0,1:T(8,128)S(1)} %broadcast_add_fusion.2, f32[128,128]{1,0:T(8,128)S(1)} %copy.77, f32[128]{0:T(128)S(1)} %get-tuple-element.245, f32[128,128]{1,0:T(8,128)} %copy.78, f32[128]{0:T(128)S(1)} %get-tuple-element.247, ...), kind=kOutput, calls=%fused_computation.9.clone.1 | convolution fusion | flops 1663041536 | bytes 625160 | tf_op jit(solution)/shard_map/while/body/eval_jaxpr/dot_general | solution.py:55
  218.0 1.2 convolution_convert_fusion.4
  226.0 11.6 %fusion.52 = f32[]{:T(128)} fusion(f32[]{:T(128)} %bitcast.138, f32[128]{0:T(128)S(1)} %fusion.50, f32[128,128]{0,1:T(8,128)S(1)} %broadcast_add_fusion.2, f32[128,128]{1,0:T(8,128)S(1)} %copy.77, f32[128]{0:T(128)S(1)} %get-tuple-element.245, f32[128,128]{1,0:T(8,128)} %copy.78, f32[128]{0:T(128)S(1)} %get-tuple-element.247, ...), kind=kOutput, calls=%fused_computation.9.clone.1 | convolution fusion | flops 1663041536 | bytes 625160 | tf_op jit(solution)/shard_map/while/body/eval_jaxpr/dot_general | solution.py:55
  239.7 1.2 convolution_convert_fusion.4
  247.7 11.6 %fusion.52 = f32[]{:T(128)} fusion(f32[]{:T(128)} %bitcast.138, f32[128]{0:T(128)S(1)} %fusion.50, f32[128,128]{0,1:T(8,128)S(1)} %broadcast_add_fusion.2, f32[128,128]{1,0:T(8,128)S(1)} %copy.77, f32[128]{0:T(128)S(1)} %get-tuple-element.245, f32[128,128]{1,0:T(8,128)} %copy.78, f32[128]{0:T(128)S(1)} %get-tuple-element.247, ...), kind=kOutput, calls=%fused_computation.9.clone.1 | convolution fusion | flops 1663041536 | bytes 625160 | tf_op jit(solution)/shard_map/while/body/eval_jaxpr/dot_general | solution.py:55
  261.4 1.2 convolution_convert_fusion.4
  269.4 11.6 %fusion.52 = f32[]{:T(128)} fusion(f32[]{:T(128)} %bitcast.138, f32[128]{0:T(128)S(1)} %fusion.50, f32[128,128]{0,1:T(8,128)S(1)} %broadcast_add_fusion.2, f32[128,128]{1,0:T(8,128)S(1)} %copy.77, f32[128]{0:T(128)S(1)} %get-tuple-element.245, f32[128,128]{1,0:T(8,128)} %copy.78, f32[128]{0:T(128)S(1)} %get-tuple-element.247, ...), kind=kOutput, calls=%fused_computation.9.clone.1 | convolution fusion | flops 1663041536 | bytes 625160 | tf_op jit(solution)/shard_map/while/body/eval_jaxpr/dot_general | solution.py:55
  283.1 1.2 convolution_convert_fusion.4
  291.1 11.6 %fusion.52 = f32[]{:T(128)} fusion(f32[]{:T(128)} %bitcast.138, f32[128]{0:T(128)S(1)} %fusion.50, f32[128,128]{0,1:T(8,128)S(1)} %broadcast_add_fusion.2, f32[128,128]{1,0:T(8,128)S(1)} %copy.77, f32[128]{0:T(128)S(1)} %get-tuple-element.245, f32[128,128]{1,0:T(8,128)} %copy.78, f32[128]{0:T(128)S(1)} %get-tuple-element.247, ...), kind=kOutput, calls=%fused_computation.9.clone.1 | convolution fusion | flops 1663041536 | bytes 625160 | tf_op jit(solution)/shard_map/while/body/eval_jaxpr/dot_general | solution.py:55
  304.8 1.2 convolution_convert_fusion.4
  312.8 11.6 %fusion.52 = f32[]{:T(128)} fusion(f32[]{:T(128)} %bitcast.138, f32[128]{0:T(128)S(1)} %fusion.50, f32[128,128]{0,1:T(8,128)S(1)} %broadcast_add_fusion.2, f32[128,128]{1,0:T(8,128)S(1)} %copy.77, f32[128]{0:T(128)S(1)} %get-tuple-element.245, f32[128,128]{1,0:T(8,128)} %copy.78, f32[128]{0:T(128)S(1)} %get-tuple-element.247, ...), kind=kOutput, calls=%fused_computation.9.clone.1 | convolution fusion | flops 1663041536 | bytes 625160 | tf_op jit(solution)/shard_map/while/body/eval_jaxpr/dot_general | solution.py:55
  325.4 39.1 %all-reduce.1 = f32[1024]{0:T(1024)S(1)} all-reduce(f32[1024]{0:T(1024)S(1)} %select_reduce_fusion), channel_id=3, replica_groups=mesh['pair'=16,'rep'=2] {'pair'}, use_global_device_ids=true, to_apply=%region_6.7.clone | all-reduce | flops 1024 | bytes 8192
  364.5 2.9 psum.7
  (243 shorter events, 96.0 us)
Async XLA Ops:
  13.7 15.5 %all-to-all-start = ((s32[16,1,3]{2,1,0:T(1,128)}), s32[16,1,3]{2,1,0:T(1,128)S(1)}, u32[]{:S(2)}, u32[]{:S(2)}) async-start(s32[16,1,3]{2,1,0:T(1,128)} %bitcast.29), calls=%async_computation | async-start | bytes 16384 | tf_op jit(solution)/shard_map/all_to_all | solution.py:111
  21.9 125.9 %all-gather.3.cloned.1.call-start = ((), (), s32[]{:S(2)}) async-start(), calls=%async_computation.2 | async-start | bytes 9437184 | tf_op jit(solution)/shard_map/all_gather | solution.py:120
  32.8 9.8 %collective-permute-start = (bf16[1,3,64,512]{3,2,1,0:T(8,128)(2,1)S(1)}, bf16[1,3,64,512]{3,2,1,0:T(8,128)(2,1)S(1)}, u32[]{:S(2)}, u32[]{:S(2)}) collective-permute-start(bf16[1,3,64,512]{3,2,1,0:T(8,128)(2,1)S(1)} %get-tuple-element.163), channel_id=1, source_target_pairs={{0,2},{2,0},{4,6},{6,4},{8,10},{10,8},{12,14},{14,12},{16,18},{18,... | collective-permute-start | bytes 589832 | tf_op jit(solution)/shard_map/ppermute | solution.py:25
  33.5 9.9 %collective-permute-start.1 = (bf16[1,3,64,512]{3,2,1,0:T(8,128)(2,1)S(1)}, bf16[1,3,64,512]{3,2,1,0:T(8,128)(2,1)S(1)}, u32[]{:S(2)}, u32[]{:S(2)}) collective-permute-start(bf16[1,3,64,512]{3,2,1,0:T(8,128)(2,1)S(1)} %get-tuple-element.162), channel_id=1, source_target_pairs={{0,4},{2,6},{4,0},{6,2},{8,12},{10,14},{12,8},{14,10},{16,20},{18,... | collective-permute-start | bytes 589832 | tf_op jit(solution)/shard_map/ppermute | solution.py:25
  34.0 12.5 %collective-permute-start.2 = (bf16[1,3,64,512]{3,2,1,0:T(8,128)(2,1)S(1)}, bf16[1,3,64,512]{3,2,1,0:T(8,128)(2,1)S(1)}, u32[]{:S(2)}, u32[]{:S(2)}) collective-permute-start(bf16[1,3,64,512]{3,2,1,0:T(8,128)(2,1)S(1)} %get-tuple-element.161), channel_id=1, source_target_pairs={{0,6},{2,4},{4,2},{6,0},{8,14},{10,12},{12,10},{14,8},{16,22},{18,... | collective-permute-start | bytes 589832 | tf_op jit(solution)/shard_map/ppermute | solution.py:25
  36.4 11.9 %collective-permute-start.3 = (bf16[1,3,64,512]{3,2,1,0:T(8,128)(2,1)S(1)}, bf16[1,3,64,512]{3,2,1,0:T(8,128)(2,1)S(1)}, u32[]{:S(2)}, u32[]{:S(2)}) collective-permute-start(bf16[1,3,64,512]{3,2,1,0:T(8,128)(2,1)S(1)} %get-tuple-element.160), channel_id=1, source_target_pairs={{0,8},{2,10},{4,12},{6,14},{8,0},{10,2},{12,4},{14,6},{16,24},{18,... | collective-permute-start | bytes 589832 | tf_op jit(solution)/shard_map/ppermute | solution.py:25
  37.0 17.5 %collective-permute-start.4 = (bf16[1,3,64,512]{3,2,1,0:T(8,128)(2,1)S(1)}, bf16[1,3,64,512]{3,2,1,0:T(8,128)(2,1)S(1)}, u32[]{:S(2)}, u32[]{:S(2)}) collective-permute-start(bf16[1,3,64,512]{3,2,1,0:T(8,128)(2,1)S(1)} %get-tuple-element.159), channel_id=1, source_target_pairs={{0,10},{2,8},{4,14},{6,12},{8,2},{10,0},{12,6},{14,4},{16,26},{18,... | collective-permute-start | bytes 589832 | tf_op jit(solution)/shard_map/ppermute | solution.py:25
  42.7 16.3 %collective-permute-start.5 = (bf16[1,3,64,512]{3,2,1,0:T(8,128)(2,1)S(1)}, bf16[1,3,64,512]{3,2,1,0:T(8,128)(2,1)S(1)}, u32[]{:S(2)}, u32[]{:S(2)}) collective-permute-start(bf16[1,3,64,512]{3,2,1,0:T(8,128)(2,1)S(1)} %get-tuple-element.158), channel_id=1, source_target_pairs={{0,12},{2,14},{4,8},{6,10},{8,4},{10,6},{12,0},{14,2},{16,28},{18,... | collective-permute-start | bytes 589832 | tf_op jit(solution)/shard_map/ppermute | solution.py:25
  43.4 20.0 %collective-permute-start.6 = (bf16[1,3,64,512]{3,2,1,0:T(8,128)(2,1)S(1)}, bf16[1,3,64,512]{3,2,1,0:T(8,128)(2,1)S(1)}, u32[]{:S(2)}, u32[]{:S(2)}) collective-permute-start(bf16[1,3,64,512]{3,2,1,0:T(8,128)(2,1)S(1)} %get-tuple-element.157), channel_id=1, source_target_pairs={{0,14},{2,12},{4,10},{6,8},{8,6},{10,4},{12,2},{14,0},{16,30},{18,... | collective-permute-start | bytes 589832 | tf_op jit(solution)/shard_map/ppermute | solution.py:25
  46.5 34.0 %collective-permute-start.7 = (bf16[1,3,64,512]{3,2,1,0:T(8,128)(2,1)S(1)}, bf16[1,3,64,512]{3,2,1,0:T(8,128)(2,1)S(1)}, u32[]{:S(2)}, u32[]{:S(2)}) collective-permute-start(bf16[1,3,64,512]{3,2,1,0:T(8,128)(2,1)S(1)} %get-tuple-element.156), channel_id=1, source_target_pairs={{0,16},{2,18},{4,20},{6,22},{8,24},{10,26},{12,28},{14,30},{16,0},... | collective-permute-start | bytes 589832 | tf_op jit(solution)/shard_map/ppermute | solution.py:25
  48.3 37.7 %collective-permute-start.8 = (bf16[1,3,64,512]{3,2,1,0:T(8,128)(2,1)S(1)}, bf16[1,3,64,512]{3,2,1,0:T(8,128)(2,1)S(1)}, u32[]{:S(2)}, u32[]{:S(2)}) collective-permute-start(bf16[1,3,64,512]{3,2,1,0:T(8,128)(2,1)S(1)} %get-tuple-element.155), channel_id=1, source_target_pairs={{0,18},{2,16},{4,22},{6,20},{8,26},{10,24},{12,30},{14,28},{16,2},... | collective-permute-start | bytes 589832 | tf_op jit(solution)/shard_map/ppermute | solution.py:25
  54.5 42.0 %collective-permute-start.9 = (bf16[1,3,64,512]{3,2,1,0:T(8,128)(2,1)S(1)}, bf16[1,3,64,512]{3,2,1,0:T(8,128)(2,1)S(1)}, u32[]{:S(2)}, u32[]{:S(2)}) collective-permute-start(bf16[1,3,64,512]{3,2,1,0:T(8,128)(2,1)S(1)} %get-tuple-element.154), channel_id=1, source_target_pairs={{0,20},{2,22},{4,16},{6,18},{8,28},{10,30},{12,24},{14,26},{16,4},... | collective-permute-start | bytes 589832 | tf_op jit(solution)/shard_map/ppermute | solution.py:25
  58.9 42.3 %collective-permute-start.10 = (bf16[1,3,64,512]{3,2,1,0:T(8,128)(2,1)S(1)}, bf16[1,3,64,512]{3,2,1,0:T(8,128)(2,1)S(1)}, u32[]{:S(2)}, u32[]{:S(2)}) collective-permute-start(bf16[1,3,64,512]{3,2,1,0:T(8,128)(2,1)S(1)} %get-tuple-element.153), channel_id=1, source_target_pairs={{0,22},{2,20},{4,18},{6,16},{8,30},{10,28},{12,26},{14,24},{16,6},... | collective-permute-start | bytes 589832 | tf_op jit(solution)/shard_map/ppermute | solution.py:25
  63.3 38.6 %collective-permute-start.11 = (bf16[1,3,64,512]{3,2,1,0:T(8,128)(2,1)S(1)}, bf16[1,3,64,512]{3,2,1,0:T(8,128)(2,1)S(1)}, u32[]{:S(2)}, u32[]{:S(2)}) collective-permute-start(bf16[1,3,64,512]{3,2,1,0:T(8,128)(2,1)S(1)} %get-tuple-element.152), channel_id=1, source_target_pairs={{0,24},{2,26},{4,28},{6,30},{8,16},{10,18},{12,20},{14,22},{16,8},... | collective-permute-start | bytes 589832 | tf_op jit(solution)/shard_map/ppermute | solution.py:25
  80.5 22.1 %collective-permute-start.12 = (bf16[1,3,64,512]{3,2,1,0:T(8,128)(2,1)S(1)}, bf16[1,3,64,512]{3,2,1,0:T(8,128)(2,1)S(1)}, u32[]{:S(2)}, u32[]{:S(2)}) collective-permute-start(bf16[1,3,64,512]{3,2,1,0:T(8,128)(2,1)S(1)} %get-tuple-element.151), channel_id=1, source_target_pairs={{0,26},{2,24},{4,30},{6,28},{8,18},{10,16},{12,22},{14,20},{16,10}... | collective-permute-start | bytes 589832 | tf_op jit(solution)/shard_map/ppermute | solution.py:25
  86.0 17.3 %collective-permute-start.13 = (bf16[1,3,64,512]{3,2,1,0:T(8,128)(2,1)S(1)}, bf16[1,3,64,512]{3,2,1,0:T(8,128)(2,1)S(1)}, u32[]{:S(2)}, u32[]{:S(2)}) collective-permute-start(bf16[1,3,64,512]{3,2,1,0:T(8,128)(2,1)S(1)} %get-tuple-element.150), channel_id=1, source_target_pairs={{0,28},{2,30},{4,24},{6,26},{8,20},{10,22},{12,16},{14,18},{16,12}... | collective-permute-start | bytes 589832 | tf_op jit(solution)/shard_map/ppermute | solution.py:25
  96.4 9.4 %collective-permute-start.14 = (bf16[1,3,64,512]{3,2,1,0:T(8,128)(2,1)S(1)}, bf16[1,3,64,512]{3,2,1,0:T(8,128)(2,1)S(1)}, u32[]{:S(2)}, u32[]{:S(2)}) collective-permute-start(bf16[1,3,64,512]{3,2,1,0:T(8,128)(2,1)S(1)} %get-tuple-element.149), channel_id=1, source_target_pairs={{0,30},{2,28},{4,26},{6,24},{8,22},{10,20},{12,18},{14,16},{16,14}... | collective-permute-start | bytes 589832 | tf_op jit(solution)/shard_map/ppermute | solution.py:25
  110.8 1.2 copy-start.2
  112.1 19.4 %copy-start.5 = (u32[32]{0:T(128)S(1)}, u32[32]{0:T(128)}, u32[]{:S(2)}) copy-start(u32[32]{0:T(128)} %constant.128) | copy-start | bytes 388
  116.4 24.9 %all-to-all-start.1 = ((bf16[16,2,6144]{2,1,0:T(2,128)(2,1)}), bf16[16,2,6144]{2,1,0:T(2,128)(2,1)S(1)}, u32[]{:S(2)}, u32[]{:S(2)}) async-start(bf16[16,2,6144]{2,1,0:T(2,128)(2,1)} %reshape.335), calls=%async_computation.1 | async-start | bytes 786432 | tf_op jit(solution)/shard_map/all_to_all | solution.py:117
  147.9 3.6 copy-start.3
  147.9 3.6 copy-start.4
  151.5 3.6 copy-start
  160.9 12.3 %copy-start.1 = (bf16[8,3,64,1024]{3,2,1,0:T(8,128)(2,1)S(1)}, bf16[8,3,64,1024]{3,2,1,0:T(8,128)(2,1)}, u32[]{:S(2)}) copy-start(bf16[8,3,64,1024]{3,2,1,0:T(8,128)(2,1)} %copy-done) | copy-start | bytes 9437188 | tf_op jit(solution)/shard_map/while
  173.2 3.6 copy-start
  182.6 12.3 %copy-start.1 = (bf16[8,3,64,1024]{3,2,1,0:T(8,128)(2,1)S(1)}, bf16[8,3,64,1024]{3,2,1,0:T(8,128)(2,1)}, u32[]{:S(2)}) copy-start(bf16[8,3,64,1024]{3,2,1,0:T(8,128)(2,1)} %copy-done) | copy-start | bytes 9437188 | tf_op jit(solution)/shard_map/while
  194.9 3.6 copy-start
  204.3 12.3 %copy-start.1 = (bf16[8,3,64,1024]{3,2,1,0:T(8,128)(2,1)S(1)}, bf16[8,3,64,1024]{3,2,1,0:T(8,128)(2,1)}, u32[]{:S(2)}) copy-start(bf16[8,3,64,1024]{3,2,1,0:T(8,128)(2,1)} %copy-done) | copy-start | bytes 9437188 | tf_op jit(solution)/shard_map/while
  216.6 3.6 copy-start
  226.0 12.3 %copy-start.1 = (bf16[8,3,64,1024]{3,2,1,0:T(8,128)(2,1)S(1)}, bf16[8,3,64,1024]{3,2,1,0:T(8,128)(2,1)}, u32[]{:S(2)}) copy-start(bf16[8,3,64,1024]{3,2,1,0:T(8,128)(2,1)} %copy-done) | copy-start | bytes 9437188 | tf_op jit(solution)/shard_map/while
  238.3 3.6 copy-start
  247.7 12.3 %copy-start.1 = (bf16[8,3,64,1024]{3,2,1,0:T(8,128)(2,1)S(1)}, bf16[8,3,64,1024]{3,2,1,0:T(8,128)(2,1)}, u32[]{:S(2)}) copy-start(bf16[8,3,64,1024]{3,2,1,0:T(8,128)(2,1)} %copy-done) | copy-start | bytes 9437188 | tf_op jit(solution)/shard_map/while
  260.0 3.6 copy-start
  269.4 12.3 %copy-start.1 = (bf16[8,3,64,1024]{3,2,1,0:T(8,128)(2,1)S(1)}, bf16[8,3,64,1024]{3,2,1,0:T(8,128)(2,1)}, u32[]{:S(2)}) copy-start(bf16[8,3,64,1024]{3,2,1,0:T(8,128)(2,1)} %copy-done) | copy-start | bytes 9437188 | tf_op jit(solution)/shard_map/while
  281.7 3.6 copy-start
  291.1 12.3 %copy-start.1 = (bf16[8,3,64,1024]{3,2,1,0:T(8,128)(2,1)S(1)}, bf16[8,3,64,1024]{3,2,1,0:T(8,128)(2,1)}, u32[]{:S(2)}) copy-start(bf16[8,3,64,1024]{3,2,1,0:T(8,128)(2,1)} %copy-done) | copy-start | bytes 9437188 | tf_op jit(solution)/shard_map/while
  303.4 3.6 copy-start
  312.8 12.3 %copy-start.1 = (bf16[8,3,64,1024]{3,2,1,0:T(8,128)(2,1)S(1)}, bf16[8,3,64,1024]{3,2,1,0:T(8,128)(2,1)}, u32[]{:S(2)}) copy-start(bf16[8,3,64,1024]{3,2,1,0:T(8,128)(2,1)} %copy-done) | copy-start | bytes 9437188 | tf_op jit(solution)/shard_map/while
  325.1 42.4 %copy-start.6 = (f32[8]{0:T(128)}, f32[8]{0:T(128)S(1)}, u32[]{:S(2)}) copy-start(f32[8]{0:T(128)S(1)} %get-tuple-element.57) | copy-start | bytes 100
Sparse Core Ops, SparseCore 0:
  111.0 26.1 all-gather.2
